TPU v7x, 128 devices: a whole 4x4x4 slice. The times are simulated.
128 devices in a mesh: ctx: 32 (over x_hi, z, y), tp: 4 (over x_lo, core).
Axes of the slice: x: 4 (x_hi: 2, x_lo: 2; x = x_hi * 2 + x_lo), y: 4, z: 4, core: 2. Of those that a mesh axis runs over, the one named last changes fastest.
Arguments:
- tokens: bfloat16 [16384, 6144], P(('ctx', 'tp')), may hold values from -18 to 18
- w_query: bfloat16 [6144, 3072], P(None, 'tp'), may hold values from -1 to 1
- key_matrix: bfloat16 [6144, 512], P(None, 'tp'), may hold values from -1 to 1
- value_matrix: bfloat16 [6144, 512], P(None, 'tp'), may hold values from -0.078125 to 0.078125
- w_out: bfloat16 [3072, 6144], P('tp'), may hold values from -0.109375 to 0.109375
- span_order: int32 [32, 2], replicated, may hold values from 0 to 63, as said below
Outputs:
- attended: bfloat16 [16384, 6144], P(('ctx', 'tp'))
Inputs may be any that keep to these rules, and one draw needn't show every extreme that they name: `span_order`: row r is (p, 63 - p) with p a permutation of 0 to 31, so every span appears once.
All inputs are finite; a program needn't handle non-finite values.
Results may differ from a plain program's by a relative error of at most 0.014.
The roundings to bfloat16 on the way count: a program that leaves them out, or rounds other values in their place, can miss the bound.
Values may be sent and summed in bfloat16 or wider, within the bound.
No kernel may reach another device: no remote copies, remote signals or barrier semaphores. Data moves between devices by JAX's collectives and lax.ppermute only.
A program may use at most 128 MiB of HBM per device.

v0:
```python
import math
import jax
import jax.numpy as jnp
from jax import lax
from jax.sharding import PartitionSpec as P

ROPE_BASE = 1000000.0


def rotary_embed(values, token_positions):
    half = values.shape[-1] // 2
    freq = ROPE_BASE ** (-(jnp.arange(half, dtype=jnp.float32) * 2.0) / values.shape[-1])
    angle = token_positions[:, None] * freq[None, :]
    cosine = jnp.cos(angle)[:, None, :]
    sine = jnp.sin(angle)[:, None, :]
    first = values[..., :half]
    second = values[..., half:]
    return jnp.concatenate(
        [first * cosine - second * sine, second * cosine + first * sine], axis=-1
    )


def body(tokens, w_query, key_matrix, value_matrix, w_out, span_order):
    rank = lax.axis_index("ctx")
    head_dim = key_matrix.shape[1]
    qcols = w_query.shape[1]
    group = qcols // head_dim
    inv_scale = 1.0 / math.sqrt(head_dim)
    piece = lax.all_gather(tokens, "tp", axis=0, tiled=True)
    projected = jnp.concatenate(
        [
            jnp.dot(piece, w_query, preferred_element_type=jnp.float32),
            jnp.dot(piece, key_matrix, preferred_element_type=jnp.float32),
            jnp.dot(piece, value_matrix, preferred_element_type=jnp.float32),
        ],
        axis=1,
    )
    block_rows = projected.shape[0]
    span = block_rows // 2
    flat = span_order.reshape(-1)
    mine = lax.dynamic_slice(span_order, (rank, jnp.int32(0)), (1, 2)).reshape(2)
    own_pos = (
        (mine[:, None] * span + jnp.arange(span, dtype=jnp.int32)[None, :])
        .reshape(-1)
        .astype(jnp.float32)
    )
    query_rows = rotary_embed(
        projected[:, :qcols].reshape(block_rows, group, head_dim), own_pos
    ).astype(jnp.bfloat16)
    key = (
        rotary_embed(
            projected[:, qcols : qcols + head_dim].reshape(block_rows, 1, head_dim), own_pos
        )
        .reshape(block_rows, head_dim)
        .astype(jnp.bfloat16)
    )
    value_rows = projected[:, qcols + head_dim :].astype(jnp.bfloat16)
    query_rows = (
        query_rows.reshape(2, span, group, head_dim)
        .transpose(0, 2, 1, 3)
        .reshape(2, group * span, head_dim)
    )
    query_pos = jnp.tile(own_pos.reshape(2, 1, span), (1, group, 1)).reshape(2, group * span)

    def update(state, query_c, pos_c, key_tile, value_tile, key_pos):
        top_old, total_old, accum_old = state
        score = (
            lax.dot_general(
                query_c, key_tile, (((1,), (1,)), ((), ())), preferred_element_type=jnp.float32
            )
            * inv_scale
        )
        keep = key_pos[None, :] <= pos_c[:, None]
        score = jnp.where(keep, score, -1e30)
        top_new = jnp.maximum(top_old, jnp.max(score, axis=1))
        weight = jnp.where(keep, jnp.exp(score - top_new[:, None]), 0.0)
        factor = jnp.exp(top_old - top_new)
        total_new = factor * total_old + jnp.sum(weight, axis=1)
        accum_new = factor[:, None] * accum_old + jnp.dot(
            weight.astype(jnp.bfloat16), value_tile, preferred_element_type=jnp.float32
        )
        return (top_new, total_new, accum_new)

    rows_q = group * span
    start_top = jnp.full((rows_q,), -1e30, jnp.float32)
    start_total = jnp.zeros((rows_q,), jnp.float32)
    start_accum = jnp.zeros((rows_q, head_dim), jnp.float32)
    initial = (start_top, start_total, start_accum, start_top, start_total, start_accum)
    key_piece = lax.all_gather(key, "ctx", axis=0, tiled=True)
    value_piece = lax.all_gather(value_rows, "ctx", axis=0, tiled=True)
    count = key_piece.shape[0]
    global_rows = jnp.arange(count, dtype=jnp.int32)
    which = (global_rows // span)[:, None] == jnp.arange(flat.shape[0], dtype=jnp.int32)[None, :]
    span_ids = jnp.sum(jnp.where(which, flat[None, :], 0), axis=1)
    key_positions = (span_ids * span + global_rows % span).astype(jnp.float32)
    tile = math.gcd(count, span)

    def one_tile(step, state):
        key_tile = lax.dynamic_slice_in_dim(key_piece, step * tile, tile, 0)
        value_tile = lax.dynamic_slice_in_dim(value_piece, step * tile, tile, 0)
        pos_tile = lax.dynamic_slice_in_dim(key_positions, step * tile, tile, 0)
        updated = []
        for half_index in range(2):
            part_state = state[3 * half_index : 3 * half_index + 3]
            query_c = query_rows[half_index]
            pos_c = query_pos[half_index]
            needed = jnp.min(pos_tile) <= jnp.max(pos_c)
            part_state = lax.cond(
                needed,
                lambda inner: update(inner, query_c, pos_c, key_tile, value_tile, pos_tile),
                lambda inner: inner,
                part_state,
            )
            updated.extend(part_state)
        return tuple(updated)

    folded = lax.fori_loop(0, count // tile, one_tile, initial)
    halves = []
    for half_index in range(2):
        total = folded[3 * half_index + 1]
        accum = folded[3 * half_index + 2]
        mixed = (accum / total[:, None]).astype(jnp.bfloat16)
        halves.append(
            mixed.reshape(group, span, head_dim).transpose(1, 0, 2).reshape(span, group * head_dim)
        )
    heads_out = jnp.concatenate(halves, axis=0)
    return lax.psum_scatter(
        jnp.dot(heads_out, w_out, preferred_element_type=jnp.float32).astype(jnp.bfloat16),
        "tp",
        scatter_dimension=0,
        tiled=True,
    )


def solution(mesh):
    return jax.shard_map(
        body,
        mesh=mesh,
        in_specs=(
            P(("ctx", "tp"), None),
            P(None, "tp"),
            P(None, "tp"),
            P(None, "tp"),
            P("tp", None),
            P(),
        ),
        out_specs=P(("ctx", "tp"), None),
        check_vma=False,
    )
```

profile of v0, /device:TPU:1, one launch (start us, length us, event | category | flops | bytes accessed | tf_op | source)
XLA Modules:
  0.0 878.5 jit_solution(16667063462873135736)
XLA Ops:
  7.3 69.3 %all-gather.5.cloned.1.call-done = bf16[512,6144]{1,0:T(8,128)(2,1)} async-done(((bf16[128,6144]{1,0:T(8,128)(2,1)}), bf16[512,6144]{1,0:T(8,128)(2,1)}) %all-gather.5.cloned.1.call-update) | async-done | bytes 6291472 | tf_op jit(solution)/shard_map/all_gather | solution.py:29
  76.6 5.2 convolution_convert_fusion.1
  82.2 5.4 convolution_bitcast_fusion
  91.7 9.7 %fusion.50 = f32[512,768]{0,1:T(8,128)S(1)} fusion(bf16[512,6144]{1,0:T(8,128)(2,1)} %all-gather.5.cloned.1.call-done, bf16[6144,768]{1,0:T(8,128)(2,1)} %param.13), kind=kOutput, calls=%fused_computation.86 | convolution fusion | flops 4831838208 | bytes 17301504 | tf_op jit(solution)/shard_map/dot_general | solution.py:32
  104.6 57.0 %all-gather.7.cloned.1.call-done = bf16[16384,128]{1,0:T(8,128)(2,1)} async-done(((bf16[512,128]{1,0:T(8,128)(2,1)}), bf16[16384,128]{1,0:T(8,128)(2,1)}) %all-gather.7.cloned.1.call-update) | async-done | bytes 4194320 | tf_op jit(solution)/shard_map/all_gather | solution.py:90
  161.7 85.1 %all-gather.9.cloned.1.call-done = bf16[16384,1,128]{0,2,1:T(8,128)(2,1)} async-done(((bf16[512,1,128]{0,2,1:T(8,128)(2,1)}), bf16[16384,1,128]{0,2,1:T(8,128)(2,1)}) %all-gather.9.cloned.1.call-update) | async-done | bytes 4194320 | tf_op jit(solution)/shard_map/all_gather | solution.py:89
  246.9 550.0 %while.25 = (s32[]{:T(128)}, f32[1536]{0:T(1024)S(1)}, f32[1536]{0:T(1024)S(1)}, f32[1536,128]{1,0:T(8,128)S(1)}, f32[1536]{0:T(1024)S(1)}, /*index=5*/f32[1536]...) while((s32[]{:T(128)}, f32[1536]{0:T(1024)S(1)}, ...), condition=%wide.region_13.14_spmd.clone, body=%wide.region_3.13_spmd.clone.sunk | while | flops 412883200 | bytes 14330351 | solution.py:117
  255.4 2.6 conditional.7
  264.0 2.6 conditional.7
  275.1 2.6 conditional.7
  292.2 2.6 conditional.7
  309.3 2.6 conditional.7
  343.5 2.6 conditional.7
  360.6 2.6 conditional.7
  394.9 2.6 conditional.7
  548.8 2.6 conditional.7
  617.2 2.6 conditional.7
  665.9 2.6 conditional.7
  700.1 2.6 conditional.6
  734.3 2.6 conditional.6
  760.0 2.6 conditional.7
  768.5 2.6 conditional.6
  797.8 10.8 %convolution_convert_fusion = bf16[512,6144]{1,0:T(8,128)(2,1)} fusion(bf16[768,6144]{1,0:T(8,128)(2,1)} %param.16, bf16[256,768]{0,1:T(8,128)(2,1)S(1)} %bitcast.60, bf16[256,768]{0,1:T(8,128)(2,1)S(1)} %bitcast.61), kind=kOutput, calls=%fused_computation.36 | convolution fusion | flops 4836556800 | bytes 16515072 | tf_op jit(solution)/shard_map/dot_general | solution.py:128
  808.7 63.3 %reduce-scatter.2.cloned.1.call-done = bf16[128,6144]{1,0:T(8,128)(2,1)} async-done(((bf16[512,6144]{1,0:T(8,128)(2,1)}), bf16[128,6144]{1,0:T(8,128)(2,1)}) %reduce-scatter.2.cloned.1.call-update) | async-done | bytes 1572880 | tf_op jit(solution)/shard_map/reduce_scatter | solution.py:127
  (997 shorter events, 516.9 us)
Async XLA Ops:
  6.5 70.0 %copy-start = (bf16[6144,128]{1,0:T(8,128)(2,1)S(1)}, bf16[6144,128]{1,0:T(8,128)(2,1)}, u32[]{:S(2)}) copy-start(bf16[6144,128]{1,0:T(8,128)(2,1)} %param.15) | copy-start | bytes 4718596
  6.5 70.0 %all-gather.5.cloned.1.call-start = ((), (), s32[]{:S(2)}) async-start(), calls=%async_computation.1 | async-start | bytes 7864320 | tf_op jit(solution)/shard_map/all_gather | solution.py:29
  7.3 74.6 %copy-start.3 = (s32[32,2]{0,1:T(2,128)S(1)}, s32[32,2]{0,1:T(2,128)}, u32[]{:S(2)}) copy-start(s32[32,2]{0,1:T(2,128)} %param.17) | copy-start | bytes 772
  7.3 154.4 %all-gather.7.cloned.1.call-start = ((), (), s32[]{:S(2)}) async-start(), calls=%async_computation.2 | async-start | bytes 4325376 | tf_op jit(solution)/shard_map/all_gather | solution.py:90
  81.8 164.9 %all-gather.9.cloned.1.call-start = ((), (), s32[]{:S(2)}) async-start(), calls=%async_computation.4 | async-start | bytes 4325376 | tf_op jit(solution)/shard_map/all_gather | solution.py:89
  82.1 6.9 copy-start.1
  88.8 783.1 %reduce-scatter.2.cloned.1.call-start = ((), (), s32[]{:S(2)}) async-start(), calls=%async_computation.3 | async-start | bytes 7864320 | tf_op jit(solution)/shard_map/reduce_scatter | solution.py:127
  102.9 144.0 %copy-start.2 = (f32[2,256]{1,0:T(2,128)S(1)}, f32[2,256]{1,0:T(2,128)}, u32[]{:S(2)}) copy-start(f32[2,256]{1,0:T(2,128)} %copy-done.1) | copy-start | bytes 6148
Sparse Core Ops, SparseCore 0:
  9.0 67.5 all-gather.4
  81.9 79.6 all-gather.6
  164.4 82.2 all-gather.8
  808.8 63.1 reduce-scatter.1
where the time goes:
time: 892 us; the launch traced here: 878 us
  waiting for transfers between devices  275 us (31%)
  loops' own time  176 us (20%)
  matrix products  173 us (19%)
  local copies, waits for them, and re-layouts  121 us (14%)
  other arithmetic  120 us (13%)
  between operations  13.3 us (1%)
    another operation x1, loops' own time, body(): folded = lax.fori_loop(0, count // tile, one_tile, initial)  170 us
    reduce_min x64, other arithmetic, one_tile(): needed = jnp.min(pos_tile) <= jnp.max(pos_c)  91 us
    dot_general x65, matrix products, update(): lax.dot_general(query_c, key_tile, (((1,), (1,)), ((), ())), preferred_el...  89.9 us
    all_gather x1, waiting for transfers between devices, body(): key_piece = lax.all_gather(key, 'ctx', axis=0, tiled=True)  85.1 us
    all_gather x1, waiting for transfers between devices, body(): piece = lax.all_gather(tokens, 'tp', axis=0, tiled=True)  69.3 us
    reduce_scatter x1, waiting for transfers between devices, body(): lax.psum_scatter(jnp.dot(heads_out, w_out, preferred_element_type=jnp.flo...  63.3 us
    dynamic_slice x128, local copies, waits for them, and re-layouts, one_tile(): key_tile = lax.dynamic_slice_in_dim(key_piece, step * tile, tile, 0)  61.1 us
    all_gather x1, waiting for transfers between devices, body(): value_piece = lax.all_gather(value_rows, 'ctx', axis=0, tiled=True)  57 us
  transfers between devices with their start and end apart: 4, of which 4 were waited for; matrix products, arithmetic and copies ran while one was open for 3% of the time, Pallas kernels for 0%

commit v1 on v0

--- a/solution.py
+++ b/solution.py
@@ -86,7 +86,9 @@
     start_total = jnp.zeros((rows_q,), jnp.float32)
     start_accum = jnp.zeros((rows_q, head_dim), jnp.float32)
     initial = (start_top, start_total, start_accum, start_top, start_total, start_accum)
-    key_piece = lax.all_gather(key, "ctx", axis=0, tiled=True)
+    key_piece = jnp.concatenate(
+        lax.all_to_all(jnp.stack([key] * lax.axis_size("ctx")), "ctx", 0, 0), axis=0
+    )
     value_piece = lax.all_gather(value_rows, "ctx", axis=0, tiled=True)
     count = key_piece.shape[0]
     global_rows = jnp.arange(count, dtype=jnp.int32)

time: 892 us -> 781 us (0.88)
  waiting for transfers between devices: 275 us -> 217 us
  local copies, waits for them, and re-layouts: 121 us -> 65 us
  starting transfers between devices: 0.12 us -> 9.32 us
    all_gather x1 -> x0, waiting for transfers between devices: 85.1 us -> none  [body(): key_piece = lax.all_gather(key, 'ctx', axis=0, tiled=True)]
    dynamic_slice x128 -> x0, local copies, waits for them, and re-layouts: 61.1 us -> none  [one_tile(): key_tile = lax.dynamic_slice_in_dim(key_piece, step * tile, tile, 0)]
    all_to_all x0 -> x1, waiting for transfers between devices: none -> 48.2 us  [body(): lax.all_to_all(jnp.stack([key] * lax.axis_size('ctx')), 'ctx', 0, 0)]
    all_gather x1, waiting for transfers between devices: 57 us -> 36.4 us  [body(): value_piece = lax.all_gather(value_rows, 'ctx', axis=0, tiled=True)]
    all_to_all x0 -> x1, starting transfers between devices: none -> 9.23 us  [body(): lax.all_to_all(jnp.stack([key] * lax.axis_size('ctx')), 'ctx', 0, 0)]
where the time goes in v1:
time: 781 us; the launch traced here: 770 us
  waiting for transfers between devices  217 us (28%)
  matrix products  173 us (22%)
  loops' own time  173 us (22%)
  other arithmetic  120 us (15%)
  local copies, waits for them, and re-layouts  65 us (8%)
  between operations  13.3 us (2%)
  starting transfers between devices  9.32 us (1%)
    another operation x1, loops' own time, body(): folded = lax.fori_loop(0, count // tile, one_tile, initial)  168 us
    reduce_min x64, other arithmetic, one_tile(): needed = jnp.min(pos_tile) <= jnp.max(pos_c)  91 us
    dot_general x65, matrix products, update(): lax.dot_general(query_c, key_tile, (((1,), (1,)), ((), ())), preferred_el...  89.9 us
    all_gather x1, waiting for transfers between devices, body(): piece = lax.all_gather(tokens, 'tp', axis=0, tiled=True)  69.3 us
    reduce_scatter x1, waiting for transfers between devices, body(): lax.psum_scatter(jnp.dot(heads_out, w_out, preferred_element_type=jnp.flo...  62.7 us
    dynamic_slice x64, local copies, waits for them, and re-layouts, one_tile(): value_tile = lax.dynamic_slice_in_dim(value_piece, step * tile, tile, 0)  56.9 us
    dot_general x65, matrix products, update(): jnp.dot(weight.astype(jnp.bfloat16), value_tile, preferred_element_type=j...  52.2 us
    all_to_all x1, waiting for transfers between devices, body(): lax.all_to_all(jnp.stack([key] * lax.axis_size('ctx')), 'ctx', 0, 0)  48.2 us
  transfers between devices with their start and end apart: 4, of which 4 were waited for; matrix products, arithmetic and copies ran while one was open for 3% of the time, Pallas kernels for 0%

profile of v1, /device:TPU:1, one launch (start us, length us, event | category | flops | bytes accessed | tf_op | source)
XLA Modules:
  0.0 770.4 jit_solution(13357899131649554722)
XLA Ops:
  7.3 69.3 %all-gather.3.cloned.1.call-done = bf16[512,6144]{1,0:T(8,128)(2,1)} async-done(((bf16[128,6144]{1,0:T(8,128)(2,1)}), bf16[512,6144]{1,0:T(8,128)(2,1)}) %all-gather.3.cloned.1.call-update) | async-done | bytes 6291472 | tf_op jit(solution)/shard_map/all_gather | solution.py:29
  76.6 5.2 convolution_convert_fusion.1
  82.1 5.0 convolution_bitcast_fusion
  87.8 2.9 stack.2
  90.7 9.2 %all-to-all-start = ((bf16[32,512,128]{2,1,0:T(8,128)(2,1)}), bf16[32,512,128]{2,1,0:T(8,128)(2,1)}, u32[]{:S(2)}, u32[]{:S(2)}) async-start(bf16[32,512,128]{2,1,0:T(8,128)(2,1)} %stack.2), calls=%async_computation | async-start | bytes 8388608 | tf_op jit(solution)/shard_map/all_to_all | solution.py:90
  102.8 9.5 %fusion.50 = f32[512,768]{0,1:T(8,128)S(1)} fusion(bf16[512,6144]{1,0:T(8,128)(2,1)} %all-gather.3.cloned.1.call-done, bf16[6144,768]{1,0:T(8,128)(2,1)} %param.13), kind=kOutput, calls=%fused_computation.86 | convolution fusion | flops 4831838208 | bytes 17301504 | tf_op jit(solution)/shard_map/dot_general | solution.py:32
  115.7 48.2 %all-to-all-done = bf16[32,512,128]{2,1,0:T(8,128)(2,1)} async-done(((bf16[32,512,128]{2,1,0:T(8,128)(2,1)}), bf16[32,512,128]{2,1,0:T(8,128)(2,1)}, u32[]{:S(2)}, u32[]{:S(2)}) %all-to-all-start) | async-done | bytes 4194336 | tf_op jit(solution)/shard_map/all_to_all | solution.py:90
  163.9 36.4 %all-gather.5.cloned.1.call-done = bf16[16384,128]{1,0:T(8,128)(2,1)} async-done(((bf16[512,128]{1,0:T(8,128)(2,1)}), bf16[16384,128]{1,0:T(8,128)(2,1)}) %all-gather.5.cloned.1.call-update) | async-done | bytes 4194320 | tf_op jit(solution)/shard_map/all_gather | solution.py:92
  200.4 488.9 %while.25 = (s32[]{:T(128)}, f32[1536]{0:T(1024)S(1)}, f32[1536]{0:T(1024)S(1)}, f32[1536,128]{1,0:T(8,128)S(1)}, f32[1536]{0:T(1024)S(1)}, /*index=5*/f32[1536]...) while((s32[]{:T(128)}, f32[1536]{0:T(1024)S(1)}, ...), condition=%wide.region_13.14_spmd.clone, body=%wide.region_3.13_spmd.clone.sunk | while | flops 412883200 | bytes 14199275 | solution.py:119
  208.0 2.6 conditional.7
  215.6 2.6 conditional.7
  316.9 2.6 conditional.7
  344.7 2.6 conditional.6
  362.5 2.6 conditional.7
  420.7 2.6 conditional.6
  453.7 2.6 conditional.7
  514.5 2.6 conditional.7
  544.9 2.6 conditional.7
  557.4 2.6 conditional.6
  572.7 2.6 conditional.7
  636.1 2.6 conditional.7
  648.7 2.6 conditional.7
  690.3 10.8 %convolution_convert_fusion = bf16[512,6144]{1,0:T(8,128)(2,1)} fusion(bf16[768,6144]{1,0:T(8,128)(2,1)} %param.16, bf16[256,768]{0,1:T(8,128)(2,1)S(1)} %bitcast.62, bf16[256,768]{0,1:T(8,128)(2,1)S(1)} %bitcast.63), kind=kOutput, calls=%fused_computation.36 | convolution fusion | flops 4836556800 | bytes 16515072 | tf_op jit(solution)/shard_map/dot_general | solution.py:130
  701.1 62.7 %reduce-scatter.2.cloned.1.call-done = bf16[128,6144]{1,0:T(8,128)(2,1)} async-done(((bf16[512,6144]{1,0:T(8,128)(2,1)}), bf16[128,6144]{1,0:T(8,128)(2,1)}) %reduce-scatter.2.cloned.1.call-update) | async-done | bytes 1572880 | tf_op jit(solution)/shard_map/reduce_scatter | solution.py:129
  (872 shorter events, 462.9 us)
Async XLA Ops:
  6.5 70.0 %copy-start = (bf16[6144,128]{1,0:T(8,128)(2,1)S(1)}, bf16[6144,128]{1,0:T(8,128)(2,1)}, u32[]{:S(2)}) copy-start(bf16[6144,128]{1,0:T(8,128)(2,1)} %param.15) | copy-start | bytes 4718596
  6.5 70.0 %all-gather.3.cloned.1.call-start = ((), (), s32[]{:S(2)}) async-start(), calls=%async_computation.2 | async-start | bytes 7864320 | tf_op jit(solution)/shard_map/all_gather | solution.py:29
  7.3 74.6 %copy-start.4 = (s32[32,2]{0,1:T(2,128)S(1)}, s32[32,2]{0,1:T(2,128)}, u32[]{:S(2)}) copy-start(s32[32,2]{0,1:T(2,128)} %param.17) | copy-start | bytes 772
  7.3 74.8 %copy-start.1 = (bf16[6144,128]{1,0:T(8,128)(2,1)S(1)}, bf16[6144,128]{1,0:T(8,128)(2,1)}, u32[]{:S(2)}) copy-start(bf16[6144,128]{1,0:T(8,128)(2,1)} %param.14) | copy-start | bytes 4718596
  7.3 193.0 %all-gather.5.cloned.1.call-start = ((), (), s32[]{:S(2)}) async-start(), calls=%async_computation.3 | async-start | bytes 4325376 | tf_op jit(solution)/shard_map/all_gather | solution.py:92
  82.1 18.1 %copy-start.2 = (f32[2,256]{1,0:T(2,128)}, f32[2,256]{1,0:T(2,128)S(1)}, u32[]{:S(2)}) copy-start(f32[2,256]{1,0:T(2,128)S(1)} %get-tuple-element.576) | copy-start | bytes 6148
  90.7 73.1 %all-to-all-start = ((bf16[32,512,128]{2,1,0:T(8,128)(2,1)}), bf16[32,512,128]{2,1,0:T(8,128)(2,1)}, u32[]{:S(2)}, u32[]{:S(2)}) async-start(bf16[32,512,128]{2,1,0:T(8,128)(2,1)} %stack.2), calls=%async_computation | async-start | bytes 8388608 | tf_op jit(solution)/shard_map/all_to_all | solution.py:90
  100.0 663.9 %reduce-scatter.2.cloned.1.call-start = ((), (), s32[]{:S(2)}) async-start(), calls=%async_computation.4 | async-start | bytes 7864320 | tf_op jit(solution)/shard_map/reduce_scatter | solution.py:129
  113.9 86.5 %copy-start.3 = (f32[2,256]{1,0:T(2,128)S(1)}, f32[2,256]{1,0:T(2,128)}, u32[]{:S(2)}) copy-start(f32[2,256]{1,0:T(2,128)} %copy-done.2) | copy-start | bytes 6148
Sparse Core Ops, SparseCore 0:
  9.0 67.5 all-gather.2
  81.9 118.2 all-gather.4
  701.2 62.5 reduce-scatter.1
